TPU v7x, 32 devices: a whole 2x2x4 slice. The times are simulated.
32 devices in a mesh: vocab: 8 (over z, y), section: 4 (over x, core).
Axes of the slice: x: 2, y: 2, z: 4, core: 2. Of those that a mesh axis runs over, the one named last changes fastest.
Arguments:
- hidden: bfloat16 [512, 8192], P('section', 'vocab'), may hold values from -2 to 2
- targets: int32 [512], replicated, may hold values from 0 to 12287
- out_weight: bfloat16 [12288, 8192], P(('vocab', 'section')), may hold values from -2 to 2
Outputs:
- token_loss: float32 [512], replicated
- weight_grad: bfloat16 [12288, 8192], P(('vocab', 'section'))
- sent_grad: bfloat16 [512, 8192], P('section', 'vocab')
All inputs are finite; a program needn't handle non-finite values.
Results may differ from a plain program's by a relative error of at most 0.0033.
Values may be sent and summed in bfloat16 or wider, within the bound.
No kernel may reach another device: no remote copies, remote signals or barrier semaphores. Data moves between devices by JAX's collectives and lax.ppermute only.
A program may use at most 128 MiB of HBM per device.

v0:
```python
import jax
import jax.numpy as jnp
from jax import lax
from jax.sharding import PartitionSpec as P


def shifted(value, axis, steps):
    count = lax.axis_size(axis)
    pairs = [(source, (source + steps) % count) for source in range(count)]
    return lax.ppermute(value, axis, pairs)


def on_device(hidden, targets, out_weight):
    columns = lax.all_gather(hidden, "vocab", axis=1, tiled=True)
    whole = lax.all_gather(columns, "section", axis=0, tiled=True)
    rows = out_weight.shape[0]
    offset = lax.axis_index(("vocab", "section")) * rows
    logits = jnp.einsum("td,vd->tv", whole, out_weight, preferred_element_type=jnp.float32)
    picked = targets[:, None] - offset == jnp.arange(rows, dtype=jnp.int32)[None, :]
    local_hit = jnp.sum(jnp.where(picked, logits, jnp.float32(0.0)), axis=1)
    local_top = jnp.max(logits, axis=1)
    top = lax.pmax(local_top, ("vocab", "section"))
    local_sum = jnp.sum(jnp.exp(logits - top[:, None]), axis=1)
    total, target_logit = lax.psum((local_sum, local_hit), ("vocab", "section"))
    token_loss = top + jnp.log(total) - target_logit
    probs = jnp.exp(logits - top[:, None]) / total[:, None]
    dlogits = (probs - picked.astype(jnp.float32)).astype(jnp.bfloat16)
    weight_grad = jnp.einsum(
        "tv,td->vd", dlogits, whole, preferred_element_type=jnp.float32
    ).astype(jnp.bfloat16)
    token_block = lax.psum_scatter(
        jnp.dot(dlogits, out_weight, preferred_element_type=jnp.float32),
        "section",
        scatter_dimension=0,
        tiled=True,
    )
    owned = lax.psum_scatter(token_block, "vocab", scatter_dimension=1, tiled=True)
    sent_grad = shifted(owned.astype(jnp.bfloat16), "section", -1)
    return (token_loss, weight_grad, sent_grad)


def solution(mesh):
    in_specs = (P("section", "vocab"), P(), P(("vocab", "section"), None))
    out_specs = (P(), P(("vocab", "section"), None), P("section", "vocab"))
    return jax.shard_map(
        on_device, mesh=mesh, in_specs=in_specs, out_specs=out_specs, check_vma=False
    )
```

profile of v0, /device:TPU:0, one launch (start us, length us, event | category | flops | bytes accessed | tf_op | source)
XLA Modules:
  0.0 455.0 jit_solution(5437715130508668706)
XLA Ops:
  7.2 0.0 all-gather.3.cloned.1.call-start
  7.2 0.7 all-gather.3.cloned.1.call-update
  7.9 0.0 all-gather.5.cloned.1.call-start
  7.9 54.0 %all-gather.3.cloned.1.call-done = bf16[128,8192]{1,0:T(8,128)(2,1)} async-done(((bf16[128,1024]{1,0:T(8,128)(2,1)}), bf16[128,8192]{1,0:T(8,128)(2,1)}) %all-gather.3.cloned.1.call-update) | async-done | bytes 2097168 | tf_op jit(solution)/shard_map/all_gather | solution.py:14
  62.0 0.0 all-gather.5.cloned.1.call-update
  62.0 0.0 reduce-scatter.3.cloned.1.call-start
  62.1 0.7 broadcast_subtract_fusion
  62.7 57.6 %all-gather.5.cloned.1.call-done = bf16[512,8192]{1,0:T(8,128)(2,1)} async-done(((bf16[128,8192]{1,0:T(8,128)(2,1)}), bf16[512,8192]{1,0:T(8,128)(2,1)}) %all-gather.5.cloned.1.call-update) | async-done | bytes 8388624 | tf_op jit(solution)/shard_map/all_gather | solution.py:15
  120.4 7.8 %fusion.2 = (f32[512]{0:T(512)S(1)}, f32[512,384]{0,1:T(8,128)S(1)}) fusion(bf16[512,8192]{1,0:T(8,128)(2,1)} %all-gather.5.cloned.1.call-done, bf16[384,8192]{1,0:T(8,128)(2,1)} %param.5), kind=kOutput, calls=%fused_computation.9 | convolution fusion | flops 3221421568 | bytes 15468544 | tf_op jit(solution)/shard_map/td,vd->tv/dot_general | solution.py:18
  128.2 39.3 %pmax.7 = f32[512]{0:T(512)S(1)} all-reduce(f32[512]{0:T(512)S(1)} %get-tuple-element.7), channel_id=1, replica_groups=mesh['vocab'=8,'section'=4] {'vocab','section'}, use_global_device_ids=true, to_apply=%region_1.2 | all-reduce | flops 512 | bytes 4096 | tf_op jit(solution)/shard_map/pmax | solution.py:22
  167.5 0.2 fusion
  167.7 40.9 %all-reduce = (f32[512]{0:T(512)S(1)}, f32[512]{0:T(512)S(1)}) all-reduce(f32[512]{0:T(512)S(1)} %get-tuple-element.4, f32[512]{0:T(512)S(1)} %get-tuple-element.3), channel_id=1, replica_groups=mesh['vocab'=8,'section'=4] {'vocab','section'}, use_global_device_ids=true, to_apply=%region_5.6 | all-reduce | flops 1024 | bytes 8192 | tf_op jit(solution)/shard_map/psum | solution.py:24
  208.7 10.9 %fusion.1 = f32[512,8192]{1,0:T(8,128)} fusion(bf16[384,8192]{1,0:T(8,128)(2,1)} %param.5, f32[512,384]{0,1:T(8,128)S(1)} %get-tuple-element.8, f32[512]{0:T(512)S(1)} %get-tuple-element.6, s32[512]{0:T(512)S(1)} %broadcast_subtract_fusion, f32[512]{0:T(512)S(1)} %pmax.7), kind=kOutput, calls=%fused_computation.8 | convolution fusion | flops 3222405120 | bytes 23861248 | tf_op jit(solution)/shard_map/dot_general | solution.py:32
  219.6 0.0 reduce-scatter.3.cloned.1.call-update
  219.6 0.0 reduce-scatter.5.cloned.1.call-start
  219.7 125.0 %reduce-scatter.3.cloned.1.call-done = f32[128,8192]{1,0:T(8,128)} async-done(((f32[512,8192]{1,0:T(8,128)}), f32[128,8192]{1,0:T(8,128)}) %reduce-scatter.3.cloned.1.call-update) | async-done | bytes 4194320 | tf_op jit(solution)/shard_map/reduce_scatter | solution.py:31
  344.6 0.0 reduce-scatter.5.cloned.1.call-update
  344.6 92.2 %reduce-scatter.5.cloned.1.call-done = f32[128,1024]{1,0:T(8,128)} async-done(((f32[128,8192]{1,0:T(8,128)}), f32[128,1024]{1,0:T(8,128)}) %reduce-scatter.5.cloned.1.call-update) | async-done | bytes 524304 | tf_op jit(solution)/shard_map/reduce_scatter | solution.py:37
  436.8 1.1 convert_element_type.15
  437.9 0.6 collective-permute-start
  438.5 8.7 %convolution_convert_fusion = bf16[384,8192]{1,0:T(8,128)(2,1)} fusion(bf16[512,8192]{1,0:T(8,128)(2,1)} %all-gather.5.cloned.1.call-done, f32[512,384]{0,1:T(8,128)S(1)} %get-tuple-element.8, f32[512]{0:T(512)S(1)} %get-tuple-element.6, s32[512]{0:T(512)S(1)} %broadcast_subtract_fusion, f32[512]{0:T(512)S(1)} %pmax.7), kind=kOutput, calls=%fused_computation | convolution fusion | flops 3225550848 | bytes 15472640 | tf_op jit(solution)/shard_map/tv,td->vd/dot_general | solution.py:28
  447.2 0.6 add_subtract_fusion
  447.8 0.0 collective-permute-done
  447.8 0.7 copy.7
Async XLA Ops:
  7.2 54.8 %all-gather.3.cloned.1.call-start = ((), (), s32[]{:S(2)}) async-start(), calls=%async_computation.2 | async-start | bytes 2359296 | tf_op jit(solution)/shard_map/all_gather | solution.py:14
  7.9 112.5 %all-gather.5.cloned.1.call-start = ((), (), s32[]{:S(2)}) async-start(), calls=%async_computation.3 | async-start | bytes 10485760 | tf_op jit(solution)/shard_map/all_gather | solution.py:15
  62.0 282.6 %reduce-scatter.3.cloned.1.call-start = ((), (), s32[]{:S(2)}) async-start(), calls=%async_computation.4 | async-start | bytes 20971520 | tf_op jit(solution)/shard_map/reduce_scatter | solution.py:31
  219.6 217.2 %reduce-scatter.5.cloned.1.call-start = ((), (), s32[]{:S(2)}) async-start(), calls=%async_computation.5 | async-start | bytes 4718592 | tf_op jit(solution)/shard_map/reduce_scatter | solution.py:37
  437.9 9.9 %collective-permute-start = (bf16[128,1024]{1,0:T(8,128)(2,1)S(1)}, bf16[128,1024]{1,0:T(8,128)(2,1)S(1)}, u32[]{:S(2)}, u32[]{:S(2)}) collective-permute-start(bf16[128,1024]{1,0:T(8,128)(2,1)S(1)} %convert_element_type.15), channel_id=1, source_target_pairs={{0,3},{1,0},{2,1},{3,2},{4,7},{5,4},{6,5},{7,6},{8,11},{9,8},{10,9... | collective-permute-start | bytes 786440 | tf_op jit(solution)/shard_map/ppermute | solution.py:10
Sparse Core Ops, SparseCore 0:
  10.2 51.7 all-gather.2
  63.5 56.7 all-gather.4
  219.7 124.8 reduce-scatter.2
  348.1 88.6 reduce-scatter.4
where the time goes:
time: 456 us; the launch traced here: 455 us
  waiting for transfers between devices  330 us (72%)
  blocking collectives  80.2 us (18%)
  matrix products  27.5 us (6%)
  between operations  13.8 us (3%)
    reduce_scatter x1, waiting for transfers between devices, on_device(): lax.psum_scatter(jnp.dot(dlogits, out_weight, preferred_element_type=jnp....  125 us
    reduce_scatter x1, waiting for transfers between devices, on_device(): lax.psum_scatter(token_block, 'vocab', scatter_dimension=1, tiled=True)  92.2 us
    all_gather x1, waiting for transfers between devices, on_device(): whole = lax.all_gather(columns, 'section', axis=0, tiled=True)  57.6 us
    all_gather x1, waiting for transfers between devices, on_device(): columns = lax.all_gather(hidden, 'vocab', axis=1, tiled=True)  54 us
    psum x1, blocking collectives, on_device(): total, target_logit = lax.psum((local_sum, local_hit), ('vocab', 'section'))  40.9 us
    pmax x1, blocking collectives, on_device(): top = lax.pmax(local_top, ('vocab', 'section'))  39.3 us
    dot_general x1, matrix products, on_device(): jnp.dot(dlogits, out_weight, preferred_element_type=jnp.float32)  10.9 us
  transfers between devices with their start and end apart: 5, of which 4 were waited for; matrix products, arithmetic and copies ran while one was open for 2% of the time, Pallas kernels for 0%

commit v1 on v0

--- a/solution.py
+++ b/solution.py
@@ -21,7 +21,7 @@
     local_top = jnp.max(logits, axis=1)
     top = lax.pmax(local_top, ("vocab", "section"))
     local_sum = jnp.sum(jnp.exp(logits - top[:, None]), axis=1)
-    total, target_logit = lax.psum((local_sum, local_hit), ("vocab", "section"))
+    total, target_logit = lax.psum(lax.psum((local_sum, local_hit), "vocab"), "section")
     token_loss = top + jnp.log(total) - target_logit
     probs = jnp.exp(logits - top[:, None]) / total[:, None]
     dlogits = (probs - picked.astype(jnp.float32)).astype(jnp.bfloat16)

time: 456 us -> 439 us (0.963)
  blocking collectives: 80.2 us -> 66 us
    psum x1 -> x2, blocking collectives: 40.9 us -> 26.7 us  [the longest x1 21.1 us: on_device(): lax.psum((local_sum, local_hit), 'vocab')]
where the time goes in v1:
time: 439 us
  waiting for transfers between devices  327 us (74%)
  blocking collectives  66 us (15%)
  matrix products  27.5 us (6%)
  between operations  13.8 us (3%)
    reduce_scatter x1, waiting for transfers between devices, on_device(): lax.psum_scatter(jnp.dot(dlogits, out_weight, preferred_element_type=jnp....  123 us
    reduce_scatter x1, waiting for transfers between devices, on_device(): lax.psum_scatter(token_block, 'vocab', scatter_dimension=1, tiled=True)  92.2 us
    all_gather x1, waiting for transfers between devices, on_device(): whole = lax.all_gather(columns, 'section', axis=0, tiled=True)  57.6 us
    all_gather x1, waiting for transfers between devices, on_device(): columns = lax.all_gather(hidden, 'vocab', axis=1, tiled=True)  54 us
    pmax x1, blocking collectives, on_device(): top = lax.pmax(local_top, ('vocab', 'section'))  39.3 us
    psum x1, blocking collectives, on_device(): lax.psum((local_sum, local_hit), 'vocab')  21.1 us
    dot_general x1, matrix products, on_device(): jnp.dot(dlogits, out_weight, preferred_element_type=jnp.float32)  10.9 us
  transfers between devices with their start and end apart: 5, of which 4 were waited for; matrix products, arithmetic and copies ran while one was open for 2% of the time, Pallas kernels for 0%

profile of v1, /device:TPU:0, one launch (start us, length us, event | category | flops | bytes accessed | tf_op | source)
XLA Modules:
  0.0 438.5 jit_solution(4416608637661241769)
XLA Ops:
  7.2 0.0 all-gather.3.cloned.1.call-start
  7.2 0.7 all-gather.3.cloned.1.call-update
  7.9 0.0 all-gather.5.cloned.1.call-start
  7.9 54.0 %all-gather.3.cloned.1.call-done = bf16[128,8192]{1,0:T(8,128)(2,1)} async-done(((bf16[128,1024]{1,0:T(8,128)(2,1)}), bf16[128,8192]{1,0:T(8,128)(2,1)}) %all-gather.3.cloned.1.call-update) | async-done | bytes 2097168 | tf_op jit(solution)/shard_map/all_gather | solution.py:14
  62.0 0.0 all-gather.5.cloned.1.call-update
  62.0 0.0 reduce-scatter.3.cloned.1.call-start
  62.1 0.7 broadcast_subtract_fusion
  62.7 57.6 %all-gather.5.cloned.1.call-done = bf16[512,8192]{1,0:T(8,128)(2,1)} async-done(((bf16[128,8192]{1,0:T(8,128)(2,1)}), bf16[512,8192]{1,0:T(8,128)(2,1)}) %all-gather.5.cloned.1.call-update) | async-done | bytes 8388624 | tf_op jit(solution)/shard_map/all_gather | solution.py:15
  120.4 7.8 %fusion.2 = (f32[512]{0:T(512)S(1)}, f32[512,384]{0,1:T(8,128)S(1)}) fusion(bf16[512,8192]{1,0:T(8,128)(2,1)} %all-gather.5.cloned.1.call-done, bf16[384,8192]{1,0:T(8,128)(2,1)} %param.5), kind=kOutput, calls=%fused_computation.9 | convolution fusion | flops 3221421568 | bytes 15468544 | tf_op jit(solution)/shard_map/td,vd->tv/dot_general | solution.py:18
  128.2 39.3 %pmax.7 = f32[512]{0:T(512)S(1)} all-reduce(f32[512]{0:T(512)S(1)} %get-tuple-element.9), channel_id=1, replica_groups=mesh['vocab'=8,'section'=4] {'vocab','section'}, use_global_device_ids=true, to_apply=%region_1.2 | all-reduce | flops 512 | bytes 4096 | tf_op jit(solution)/shard_map/pmax | solution.py:22
  167.5 0.2 fusion
  167.8 21.1 %all-reduce = (f32[512]{0:T(512)S(1)}, f32[512]{0:T(512)S(1)}) all-reduce(f32[512]{0:T(512)S(1)} %get-tuple-element.4, f32[512]{0:T(512)S(1)} %get-tuple-element.3), channel_id=1, replica_groups=mesh['vocab'=8,'section'=4] {'vocab'}, use_global_device_ids=true, to_apply=%region_6.7 | all-reduce | flops 1024 | bytes 8192 | tf_op jit(solution)/shard_map/psum | solution.py:24
  188.8 5.6 %all-reduce.1 = (f32[512]{0:T(512)S(1)}, f32[512]{0:T(512)S(1)}) all-reduce(f32[512]{0:T(512)S(1)} %get-tuple-element.5, f32[512]{0:T(512)S(1)} %get-tuple-element.6), channel_id=1, replica_groups=mesh['vocab'=8,'section'=4] {'section'}, use_global_device_ids=true, to_apply=%region_7.8 | all-reduce | flops 1024 | bytes 8192 | tf_op jit(solution)/shard_map/psum | solution.py:24
  194.5 10.9 %fusion.1 = f32[512,8192]{1,0:T(8,128)} fusion(bf16[384,8192]{1,0:T(8,128)(2,1)} %param.5, f32[512,384]{0,1:T(8,128)S(1)} %get-tuple-element.10, f32[512]{0:T(512)S(1)} %get-tuple-element.8, s32[512]{0:T(512)S(1)} %broadcast_subtract_fusion, f32[512]{0:T(512)S(1)} %pmax.7), kind=kOutput, calls=%fused_computation.8 | convolution fusion | flops 3222405120 | bytes 23861248 | tf_op jit(solution)/shard_map/dot_general | solution.py:32
  205.4 0.0 reduce-scatter.3.cloned.1.call-update
  205.4 0.0 reduce-scatter.5.cloned.1.call-start
  205.5 122.7 %reduce-scatter.3.cloned.1.call-done = f32[128,8192]{1,0:T(8,128)} async-done(((f32[512,8192]{1,0:T(8,128)}), f32[128,8192]{1,0:T(8,128)}) %reduce-scatter.3.cloned.1.call-update) | async-done | bytes 4194320 | tf_op jit(solution)/shard_map/reduce_scatter | solution.py:31
  328.1 0.0 reduce-scatter.5.cloned.1.call-update
  328.1 92.2 %reduce-scatter.5.cloned.1.call-done = f32[128,1024]{1,0:T(8,128)} async-done(((f32[128,8192]{1,0:T(8,128)}), f32[128,1024]{1,0:T(8,128)}) %reduce-scatter.5.cloned.1.call-update) | async-done | bytes 524304 | tf_op jit(solution)/shard_map/reduce_scatter | solution.py:37
  420.3 1.1 convert_element_type.15
  421.4 0.6 collective-permute-start
  422.0 8.7 %convolution_convert_fusion = bf16[384,8192]{1,0:T(8,128)(2,1)} fusion(bf16[512,8192]{1,0:T(8,128)(2,1)} %all-gather.5.cloned.1.call-done, f32[512,384]{0,1:T(8,128)S(1)} %get-tuple-element.10, f32[512]{0:T(512)S(1)} %get-tuple-element.8, s32[512]{0:T(512)S(1)} %broadcast_subtract_fusion, f32[512]{0:T(512)S(1)} %pmax.7), kind=kOutput, calls=%fused_computation | convolution fusion | flops 3225550848 | bytes 15472640 | tf_op jit(solution)/shard_map/tv,td->vd/dot_general | solution.py:28
  430.7 0.6 add_subtract_fusion
  431.3 0.0 collective-permute-done
  431.3 0.7 copy.7
Async XLA Ops:
  7.2 54.8 %all-gather.3.cloned.1.call-start = ((), (), s32[]{:S(2)}) async-start(), calls=%async_computation.2 | async-start | bytes 2359296 | tf_op jit(solution)/shard_map/all_gather | solution.py:14
  7.9 112.5 %all-gather.5.cloned.1.call-start = ((), (), s32[]{:S(2)}) async-start(), calls=%async_computation.3 | async-start | bytes 10485760 | tf_op jit(solution)/shard_map/all_gather | solution.py:15
  62.0 266.1 %reduce-scatter.3.cloned.1.call-start = ((), (), s32[]{:S(2)}) async-start(), calls=%async_computation.4 | async-start | bytes 20971520 | tf_op jit(solution)/shard_map/reduce_scatter | solution.py:31
  205.4 214.9 %reduce-scatter.5.cloned.1.call-start = ((), (), s32[]{:S(2)}) async-start(), calls=%async_computation.5 | async-start | bytes 4718592 | tf_op jit(solution)/shard_map/reduce_scatter | solution.py:37
  421.4 9.9 %collective-permute-start = (bf16[128,1024]{1,0:T(8,128)(2,1)S(1)}, bf16[128,1024]{1,0:T(8,128)(2,1)S(1)}, u32[]{:S(2)}, u32[]{:S(2)}) collective-permute-start(bf16[128,1024]{1,0:T(8,128)(2,1)S(1)} %convert_element_type.15), channel_id=1, source_target_pairs={{0,3},{1,0},{2,1},{3,2},{4,7},{5,4},{6,5},{7,6},{8,11},{9,8},{10,9... | collective-permute-start | bytes 786440 | tf_op jit(solution)/shard_map/ppermute | solution.py:10
Sparse Core Ops, SparseCore 0:
  10.2 51.7 all-gather.2
  63.5 56.7 all-gather.4
  205.5 122.5 reduce-scatter.2
  331.6 88.6 reduce-scatter.4
